TPU v7x, 512 devices: a whole 4x4x16 slice. The times are simulated.
512 devices in a mesh: tok: 16 (over z_hi, y), feat: 32 (over x, z_lo, core).
Axes of the slice: x: 4, y: 4, z: 16 (z_hi: 4, z_lo: 4; z = z_hi * 4 + z_lo), core: 2. Of those that a mesh axis runs over, the one named last changes fastest.
Arguments:
- tokens: bfloat16 [1024, 8192], P('tok', 'feat'), may hold values from -6 to 6
- gain: float32 [8192], replicated, may hold values from 0.1 to 1.9
- proj: bfloat16 [8192, 8192], P('tok', 'feat'), may hold values from -0.0625 to 0.0625
- panel_index: int32 [1], replicated, may hold values from 0 to 31
Outputs:
- panel_rows: float32 [256, 8192], P(None, 'feat')
- solved_cross: float32 [256, 8192], P(None, 'feat')
All inputs are finite; a program needn't handle non-finite values.
Results may differ from a plain program's by a relative error of at most 0.01.
Values may be sent and summed in bfloat16 or wider, within the bound.
No kernel may reach another device: no remote copies, remote signals or barrier semaphores. Data moves between devices by JAX's collectives and lax.ppermute only.
A program may use at most 64 MiB of HBM per device.

v0:
```python
import math
import jax
import jax.numpy as jnp
from jax import lax
from jax.sharding import PartitionSpec as P

D = 8192
PANEL = 256


def solve_pair(factor, gram_part, cross_part):
    first = lax.linalg.triangular_solve(factor, gram_part, left_side=True, lower=True)
    second = lax.linalg.triangular_solve(factor, cross_part, left_side=True, lower=True)
    return (first, second)


def body(tokens, gain, proj, panel_index):
    token_full = lax.all_gather(tokens, "feat", axis=1, tiled=True)
    wide_rows = token_full.astype(jnp.float32)
    inv_rms = lax.rsqrt(jnp.mean(wide_rows * wide_rows, axis=1, keepdims=True) + 1e-05)
    normed = (wide_rows * inv_rms * gain[None, :]).astype(jnp.bfloat16)
    local_cols = tokens.shape[1]
    projected = jnp.dot(
        normed, lax.all_gather(proj, "tok", axis=0, tiled=True), preferred_element_type=jnp.float32
    )
    own_values = tokens.astype(jnp.float32)
    outputs = (own_values + projected).astype(jnp.bfloat16)
    change = (outputs.astype(jnp.float32) - own_values).astype(jnp.bfloat16)
    band_start = panel_index[0] * PANEL
    band_cols = lax.dynamic_slice_in_dim(token_full, band_start, PANEL, 1)
    gram_part = jnp.dot(band_cols.T, tokens, preferred_element_type=jnp.float32)
    cross_part = jnp.dot(band_cols.T, change, preferred_element_type=jnp.float32)
    gram_sum, cross_sum = (
        lax.psum_scatter(gram_part, "tok", scatter_dimension=0, tiled=True),
        lax.psum_scatter(cross_part, "tok", scatter_dimension=0, tiled=True),
    )
    tok_count = lax.axis_size("tok")
    feat_count = lax.axis_size("feat")
    token_count = tokens.shape[0] * tok_count
    rows_here = gram_sum.shape[0]
    row_ids = lax.broadcasted_iota(jnp.int32, gram_sum.shape, 0) + lax.axis_index("tok") * rows_here
    col_ids = (
        lax.broadcasted_iota(jnp.int32, gram_sum.shape, 1) + lax.axis_index("feat") * local_cols
    )
    ridge_mask = jnp.where(col_ids == row_ids + band_start, 0.1, 0.0).astype(jnp.float32)
    gram_rows = gram_sum / token_count + ridge_mask
    cross_rows = cross_sum * (math.sqrt(D) / token_count)
    slab_rows = PANEL // feat_count
    own_slab = lax.dynamic_slice_in_dim(band_cols, lax.axis_index("feat") * slab_rows, slab_rows, 1)
    partial_value = jnp.dot(own_slab.T, band_cols, preferred_element_type=jnp.float32)
    summed = lax.psum(partial_value, "tok")
    diag_sum = lax.all_gather(summed, "feat", axis=0, tiled=True)
    diag_block = diag_sum / token_count + 0.1 * jnp.eye(PANEL, dtype=jnp.float32)
    factor = jnp.linalg.cholesky(diag_block)
    gram_all, cross_all = (
        lax.all_gather(gram_rows, "tok", axis=0, tiled=True),
        lax.all_gather(cross_rows, "tok", axis=0, tiled=True),
    )
    panel_rows, solved_cross = solve_pair(factor, gram_all, cross_all)
    return (panel_rows, solved_cross)


def solution(mesh):
    return jax.shard_map(
        body,
        mesh=mesh,
        in_specs=(P("tok", "feat"), P(), P("tok", "feat"), P()),
        out_specs=(P(None, "feat"), P(None, "feat")),
        check_vma=False,
    )
```

profile of v0, /device:TPU:6, one launch (start us, length us, event | category | flops | bytes accessed | tf_op | source)
XLA Modules:
  0.0 510.4 jit_solution(6681423414111467340)
XLA Ops:
  7.2 0.7 all-gather.3.cloned.1.call-update
  8.6 70.5 %all-gather.3.cloned.1.call-done = bf16[64,8192]{1,0:T(8,128)(2,1)} async-done(((bf16[64,256]{1,0:T(8,128)(2,1)}), bf16[64,8192]{1,0:T(8,128)(2,1)}) %all-gather.3.cloned.1.call-update) | async-done | bytes 1048592 | tf_op jit(solution)/shard_map/all_gather | solution.py:18
  79.0 1.7 fusion.28
  80.8 0.7 all-gather.5.cloned.1.call-update
  81.6 1.1 fusion.30
  82.7 53.7 %psum.7 = f32[8,256]{1,0:T(8,128)S(1)} all-reduce(f32[8,256]{1,0:T(8,128)S(1)} %fusion.30), channel_id=1, replica_groups=mesh['tok'=16,'feat'=32] {'tok'}, use_global_device_ids=true, to_apply=%region_0.0 | all-reduce | flops 2048 | bytes 16384 | tf_op jit(solution)/shard_map/psum | solution.py:51
  136.4 36.4 %all_gather.16 = f32[256,256]{1,0:T(8,128)S(1)} all-gather(f32[8,256]{1,0:T(8,128)S(1)} %psum.7), channel_id=1, replica_groups=mesh['tok'=16,'feat'=32] {'feat'}, dimensions={0}, use_global_device_ids=true | all-gather | bytes 270336 | tf_op jit(solution)/shard_map/all_gather | solution.py:52
  173.2 11.7 %cholesky.49 = f32[128,128]{1,0:T(8,128)S(1)} custom-call(f32[128,128]{1,0:T(8,128)S(1)} %cholesky.115), custom_call_target="Cholesky" | custom-call | tf_op jit(solution)/shard_map/jit(cholesky)/cholesky | solution.py:54
  185.0 9.8 %custom-call.14 = f32[1,128,128]{1,2,0:T(8,128)S(1)} custom-call(f32[1,128,128]{2,1,0:T(8,128)S(1)} %get-tuple-element.46), custom_call_target="InvertDiagBlocksLowerTriangular" | custom-call | tf_op jit(solution)/shard_map/jit(cholesky)/cholesky | solution.py:54
  195.4 11.7 %cholesky.103 = f32[128,128]{1,0:T(8,128)S(1)} custom-call(f32[128,128]{1,0:T(8,128)S(1)} %convolution_subtract_fusion.2), custom_call_target="Cholesky" | custom-call | tf_op jit(solution)/shard_map/jit(cholesky)/cholesky | solution.py:54
  207.3 0.7 compare_reduce_fusion
  209.5 4.5 while.4
  210.3 1.4 dynamic-slice.9
  212.5 1.4 dynamic-slice.9
  214.0 19.7 %custom-call.16 = f32[2,128,128]{1,2,0:T(8,128)S(1)} custom-call(f32[2,128,128]{2,1,0:T(8,128)S(1)} %get-tuple-element.17), custom_call_target="InvertDiagBlocksLowerTriangular" | custom-call | tf_op jit(solution)/shard_map/triangular_solve/custom-call.0 | solution.py:12
  234.0 0.8 select_add_fusion.1
  234.8 67.7 %all_gather.17 = f32[256,256]{1,0:T(8,128)S(1)} all-gather(f32[16,256]{1,0:T(8,128)S(1)} %select_add_fusion.1), channel_id=1, replica_groups=mesh['tok'=16,'feat'=32] {'tok'}, dimensions={0}, use_global_device_ids=true | all-gather | bytes 278528 | tf_op jit(solution)/shard_map/all_gather | solution.py:56
  302.9 24.7 %all-gather.5.cloned.1.call-done = bf16[8192,256]{1,0:T(8,128)(2,1)} async-done(((bf16[512,256]{1,0:T(8,128)(2,1)}), bf16[8192,256]{1,0:T(8,128)(2,1)}) %all-gather.5.cloned.1.call-update) | async-done | bytes 4194320 | tf_op jit(solution)/shard_map/all_gather | solution.py:24
  327.6 4.0 fusion.7
  332.3 0.7 pad_maximum_fusion
  333.0 115.6 %reduce-scatter.5.cloned.1.call-done = f32[16,256]{1,0:T(8,128)} async-done(((f32[256,256]{1,0:T(8,128)}), f32[16,256]{1,0:T(8,128)}) %reduce-scatter.5.cloned.1.call-update) | async-done | bytes 16400 | tf_op jit(solution)/shard_map/reduce_scatter | solution.py:35
  448.6 0.7 broadcast_multiply_fusion
  449.3 52.8 %all_gather.19 = f32[256,256]{1,0:T(8,128)S(1)} all-gather(f32[16,256]{1,0:T(8,128)S(1)} %broadcast_multiply_fusion), channel_id=1, replica_groups=mesh['tok'=16,'feat'=32] {'tok'}, dimensions={0}, use_global_device_ids=true | all-gather | bytes 278528 | tf_op jit(solution)/shard_map/all_gather | solution.py:57
  503.1 0.7 pad_maximum_fusion.1
  (50 shorter events, 5.1 us)
Async XLA Ops:
  7.2 71.9 %all-gather.3.cloned.1.call-start = ((), (), s32[]{:S(2)}) async-start(), calls=%async_computation.2 | async-start | bytes 1081344 | tf_op jit(solution)/shard_map/all_gather | solution.py:18
  7.9 226.1 %reduce-scatter.3.cloned.1.call-start = ((), (), s32[]{:S(2)}) async-start(), calls=%async_computation.3 | async-start | bytes 278528 | tf_op jit(solution)/shard_map/reduce_scatter | solution.py:34
  80.8 246.8 %all-gather.5.cloned.1.call-start = ((), (), s32[]{:S(2)}) async-start(), calls=%async_computation.4 | async-start | bytes 4456448 | tf_op jit(solution)/shard_map/all_gather | solution.py:24
  81.5 367.1 %reduce-scatter.5.cloned.1.call-start = ((), (), s32[]{:S(2)}) async-start(), calls=%async_computation.5 | async-start | bytes 278528 | tf_op jit(solution)/shard_map/reduce_scatter | solution.py:35
  185.0 48.7 %copy-start = (bf16[64,8192]{1,0:T(8,128)(2,1)S(1)}, bf16[64,8192]{1,0:T(8,128)(2,1)}, u32[]{:S(2)}) copy-start(bf16[64,8192]{1,0:T(8,128)(2,1)} %all-gather.3.cloned.1.call-done) | copy-start | bytes 3145732
  209.4 118.2 %copy-start.1 = (bf16[64,256]{1,0:T(8,128)(2,1)S(1)}, bf16[64,256]{1,0:T(8,128)(2,1)}, u32[]{:S(2)}) copy-start(bf16[64,256]{1,0:T(8,128)(2,1)} %param.6) | copy-start | bytes 98308
  209.4 118.2 %copy-start.2 = (f32[8192]{0:T(1024)S(1)}, f32[8192]{0:T(1024)}, u32[]{:S(2)}) copy-start(f32[8192]{0:T(1024)} %param.7) | copy-start | bytes 98308
Sparse Core Ops, SparseCore 0:
  10.0 68.9 all-gather.2
  83.7 113.0 reduce-scatter.2
  199.7 127.8 all-gather.4
  332.1 116.5 reduce-scatter.4
where the time goes:
time: 511 us; the launch traced here: 510 us
  waiting for transfers between devices  212 us (41%)
  blocking collectives  211 us (41%)
  other arithmetic  57.1 us (11%)
  between operations  16 us (3%)
  matrix products  9.1 us (2%)
    reduce_scatter x1, waiting for transfers between devices, body(): lax.psum_scatter(cross_part, 'tok', scatter_dimension=0, tiled=True)  116 us
    all_gather x1, waiting for transfers between devices, body(): token_full = lax.all_gather(tokens, 'feat', axis=1, tiled=True)  70.5 us
    all_gather x1, blocking collectives, body(): lax.all_gather(gram_rows, 'tok', axis=0, tiled=True)  67.7 us
    psum x1, blocking collectives, body(): summed = lax.psum(partial_value, 'tok')  53.7 us
    all_gather x1, blocking collectives, body(): lax.all_gather(cross_rows, 'tok', axis=0, tiled=True)  52.8 us
    all_gather x1, blocking collectives, body(): diag_sum = lax.all_gather(summed, 'feat', axis=0, tiled=True)  36.4 us
    another operation x6, other arithmetic, body(): factor = jnp.linalg.cholesky(diag_block)  34 us
    all_gather x1, waiting for transfers between devices, body(): lax.all_gather(proj, 'tok', axis=0, tiled=True)  24.7 us
  transfers between devices with their start and end apart: 4, of which 3 were waited for; matrix products, arithmetic and copies ran while one was open for 12% of the time, Pallas kernels for 0%

commit v1 on v0

--- a/solution.py
+++ b/solution.py
@@ -6,6 +6,13 @@
 
 D = 8192
 PANEL = 256
+
+
+def all_by_exchange(x, name, dim):
+    peers = lax.axis_size(name)
+    blocks = jnp.stack([x for _ in range(peers)])
+    blocks = lax.all_to_all(blocks, name, split_axis=0, concat_axis=0)
+    return jnp.concatenate(blocks, axis=dim)
 
 
 def solve_pair(factor, gram_part, cross_part):
@@ -54,7 +61,7 @@
     factor = jnp.linalg.cholesky(diag_block)
     gram_all, cross_all = (
         lax.all_gather(gram_rows, "tok", axis=0, tiled=True),
-        lax.all_gather(cross_rows, "tok", axis=0, tiled=True),
+        all_by_exchange(cross_rows, "tok", 0),
     )
     panel_rows, solved_cross = solve_pair(factor, gram_all, cross_all)
     return (panel_rows, solved_cross)

time: 511 us -> 529 us (1.035)
  waiting for transfers between devices: 212 us -> 265 us
  blocking collectives: 211 us -> 169 us
  starting transfers between devices: 0.15 us -> 7.98 us
    reduce_scatter x1, waiting for transfers between devices: 0.02 us -> 103 us  [body(): lax.psum_scatter(gram_part, 'tok', scatter_dimension=0, tiled=True)]
    all_gather x1 -> x0, blocking collectives: 52.8 us -> none  [body(): lax.all_gather(cross_rows, 'tok', axis=0, tiled=True)]
    reduce_scatter x1, waiting for transfers between devices: 116 us -> 90.3 us  [body(): lax.psum_scatter(cross_part, 'tok', scatter_dimension=0, tiled=True)]
    all_gather x1, waiting for transfers between devices: 24.7 us -> 0.02 us  [body(): lax.all_gather(proj, 'tok', axis=0, tiled=True)]
    all_gather x1, blocking collectives: 36.4 us -> 58.4 us  [body(): diag_sum = lax.all_gather(summed, 'feat', axis=0, tiled=True)]
    all_gather x1, blocking collectives: 67.7 us -> 52.8 us  [body(): lax.all_gather(gram_rows, 'tok', axis=0, tiled=True)]
    all_to_all x0 -> x1, starting transfers between devices: none -> 7.65 us  [all_by_exchange(): blocks = lax.all_to_all(blocks, name, split_axis=0, concat_axis=0)]
  transfers between devices with their start and end apart: 4 -> 5, of which waited for: 3 -> 3; matrix products, arithmetic and copies ran while one was open for 12% -> 12% of each run, Pallas kernels for 0% -> 0%
where the time goes in v1:
time: 529 us; the launch traced here: 528 us
  waiting for transfers between devices  265 us (50%)
  blocking collectives  169 us (32%)
  other arithmetic  57 us (11%)
  between operations  15.9 us (3%)
  matrix products  8.4 us (2%)
  starting transfers between devices  7.98 us (2%)
  local copies, waits for them, and re-layouts  5.31 us (1%)
    reduce_scatter x1, waiting for transfers between devices, body(): lax.psum_scatter(gram_part, 'tok', scatter_dimension=0, tiled=True)  103 us
    reduce_scatter x1, waiting for transfers between devices, body(): lax.psum_scatter(cross_part, 'tok', scatter_dimension=0, tiled=True)  90.3 us
    all_gather x1, waiting for transfers between devices, body(): token_full = lax.all_gather(tokens, 'feat', axis=1, tiled=True)  69.6 us
    all_gather x1, blocking collectives, body(): diag_sum = lax.all_gather(summed, 'feat', axis=0, tiled=True)  58.4 us
    psum x1, blocking collectives, body(): summed = lax.psum(partial_value, 'tok')  57.5 us
    all_gather x1, blocking collectives, body(): lax.all_gather(gram_rows, 'tok', axis=0, tiled=True)  52.8 us
    another operation x6, other arithmetic, body(): factor = jnp.linalg.cholesky(diag_block)  34 us
    another operation x5, other arithmetic, solve_pair(): lax.linalg.triangular_solve(factor, gram_part, left_side=True, lower=True)  20.4 us
  transfers between devices with their start and end apart: 5, of which 3 were waited for; matrix products, arithmetic and copies ran while one was open for 12% of the time, Pallas kernels for 0%

profile of v1, /device:TPU:6, one launch (start us, length us, event | category | flops | bytes accessed | tf_op | source)
XLA Modules:
  0.0 528.1 jit_solution(9881522464720458874)
XLA Ops:
  7.2 0.7 all-gather.3.cloned.1.call-update
  7.9 0.7 all-gather.5.cloned.1.call-update
  9.4 69.6 %all-gather.3.cloned.1.call-done = bf16[64,8192]{1,0:T(8,128)(2,1)} async-done(((bf16[64,256]{1,0:T(8,128)(2,1)}), bf16[64,8192]{1,0:T(8,128)(2,1)}) %all-gather.3.cloned.1.call-update) | async-done | bytes 1048592 | tf_op jit(solution)/shard_map/all_gather | solution.py:25
  79.0 1.1 fusion.30
  80.2 57.5 %psum.7 = f32[8,256]{1,0:T(8,128)S(1)} all-reduce(f32[8,256]{1,0:T(8,128)S(1)} %fusion.30), channel_id=1, replica_groups=mesh['tok'=16,'feat'=32] {'tok'}, use_global_device_ids=true, to_apply=%region_0.0 | all-reduce | flops 2048 | bytes 16384 | tf_op jit(solution)/shard_map/psum | solution.py:58
  137.7 58.4 %all_gather.13 = f32[256,256]{1,0:T(8,128)S(1)} all-gather(f32[8,256]{1,0:T(8,128)S(1)} %psum.7), channel_id=1, replica_groups=mesh['tok'=16,'feat'=32] {'feat'}, dimensions={0}, use_global_device_ids=true | all-gather | bytes 270336 | tf_op jit(solution)/shard_map/all_gather | solution.py:59
  196.4 11.7 %cholesky.49 = f32[128,128]{1,0:T(8,128)S(1)} custom-call(f32[128,128]{1,0:T(8,128)S(1)} %cholesky.115), custom_call_target="Cholesky" | custom-call | tf_op jit(solution)/shard_map/jit(cholesky)/cholesky | solution.py:61
  208.3 9.8 %custom-call.14 = f32[1,128,128]{1,2,0:T(8,128)S(1)} custom-call(f32[1,128,128]{2,1,0:T(8,128)S(1)} %get-tuple-element.46), custom_call_target="InvertDiagBlocksLowerTriangular" | custom-call | tf_op jit(solution)/shard_map/jit(cholesky)/cholesky | solution.py:61
  218.8 4.0 fusion.7
  223.3 11.7 %cholesky.103 = f32[128,128]{1,0:T(8,128)S(1)} custom-call(f32[128,128]{1,0:T(8,128)S(1)} %convolution_subtract_fusion.2), custom_call_target="Cholesky" | custom-call | tf_op jit(solution)/shard_map/jit(cholesky)/cholesky | solution.py:61
  235.1 0.9 fusion.28
  238.1 4.0 while.4
  238.7 1.3 dynamic-slice.9
  240.7 1.3 dynamic-slice.9
  242.1 19.7 %custom-call.16 = f32[2,128,128]{1,2,0:T(8,128)S(1)} custom-call(f32[2,128,128]{2,1,0:T(8,128)S(1)} %get-tuple-element.17), custom_call_target="InvertDiagBlocksLowerTriangular" | custom-call | tf_op jit(solution)/shard_map/triangular_solve/custom-call.0 | solution.py:19
  261.8 90.3 %reduce-scatter.5.cloned.1.call-done = f32[16,256]{1,0:T(8,128)} async-done(((f32[256,256]{1,0:T(8,128)}), f32[16,256]{1,0:T(8,128)}) %reduce-scatter.5.cloned.1.call-update) | async-done | bytes 16400 | tf_op jit(solution)/shard_map/reduce_scatter | solution.py:42
  352.1 0.7 broadcast_multiply_fusion
  352.8 0.7 stack.2
  353.6 7.6 %all-to-all-start = ((f32[16,16,256]{2,1,0:T(8,128)}), f32[16,16,256]{2,1,0:T(8,128)S(1)}, u32[]{:S(2)}, u32[]{:S(2)}) async-start(f32[16,16,256]{2,1,0:T(8,128)} %stack.2), calls=%async_computation.2 | async-start | bytes 524288 | tf_op jit(solution)/shard_map/all_to_all | solution.py:14
  361.2 103.5 %reduce-scatter.3.cloned.1.call-done = f32[16,256]{1,0:T(8,128)} async-done(((f32[256,256]{1,0:T(8,128)}), f32[16,256]{1,0:T(8,128)}) %reduce-scatter.3.cloned.1.call-update) | async-done | bytes 16400 | tf_op jit(solution)/shard_map/reduce_scatter | solution.py:41
  464.7 0.8 select_add_fusion.1
  465.5 52.8 %all_gather.14 = f32[256,256]{1,0:T(8,128)S(1)} all-gather(f32[16,256]{1,0:T(8,128)S(1)} %select_add_fusion.1), channel_id=1, replica_groups=mesh['tok'=16,'feat'=32] {'tok'}, dimensions={0}, use_global_device_ids=true | all-gather | bytes 278528 | tf_op jit(solution)/shard_map/all_gather | solution.py:63
  519.2 0.7 pad_maximum_fusion
  520.9 0.7 pad_maximum_fusion.1
  (52 shorter events, 5.9 us)
Async XLA Ops:
  7.2 71.9 %all-gather.3.cloned.1.call-start = ((), (), s32[]{:S(2)}) async-start(), calls=%async_computation.3 | async-start | bytes 1081344 | tf_op jit(solution)/shard_map/all_gather | solution.py:25
  7.9 210.8 %all-gather.5.cloned.1.call-start = ((), (), s32[]{:S(2)}) async-start(), calls=%async_computation.5 | async-start | bytes 4456448 | tf_op jit(solution)/shard_map/all_gather | solution.py:31
  8.6 343.5 %reduce-scatter.5.cloned.1.call-start = ((), (), s32[]{:S(2)}) async-start(), calls=%async_computation.6 | async-start | bytes 278528 | tf_op jit(solution)/shard_map/reduce_scatter | solution.py:42
  79.0 139.3 %copy-start = (bf16[64,8192]{1,0:T(8,128)(2,1)S(1)}, bf16[64,8192]{1,0:T(8,128)(2,1)}, u32[]{:S(2)}) copy-start(bf16[64,8192]{1,0:T(8,128)(2,1)} %all-gather.3.cloned.1.call-done) | copy-start | bytes 3145732
  196.0 22.7 %copy-start.1 = (bf16[64,256]{1,0:T(8,128)(2,1)S(1)}, bf16[64,256]{1,0:T(8,128)(2,1)}, u32[]{:S(2)}) copy-start(bf16[64,256]{1,0:T(8,128)(2,1)} %param.6) | copy-start | bytes 98308
  196.0 22.7 %copy-start.2 = (f32[8192]{0:T(1024)S(1)}, f32[8192]{0:T(1024)}, u32[]{:S(2)}) copy-start(f32[8192]{0:T(1024)} %param.7) | copy-start | bytes 98308
  222.8 241.9 %reduce-scatter.3.cloned.1.call-start = ((), (), s32[]{:S(2)}) async-start(), calls=%async_computation.4 | async-start | bytes 278528 | tf_op jit(solution)/shard_map/reduce_scatter | solution.py:41
  353.6 166.4 %all-to-all-start = ((f32[16,16,256]{2,1,0:T(8,128)}), f32[16,16,256]{2,1,0:T(8,128)S(1)}, u32[]{:S(2)}, u32[]{:S(2)}) async-start(f32[16,16,256]{2,1,0:T(8,128)} %stack.2), calls=%async_computation.2 | async-start | bytes 524288 | tf_op jit(solution)/shard_map/all_to_all | solution.py:14
Sparse Core Ops, SparseCore 0:
  10.0 68.9 all-gather.2
  82.1 130.5 all-gather.4
  222.9 129.1 reduce-scatter.4
  356.6 108.0 reduce-scatter.2
